TPU v7x, 32 devices: a whole 2x2x4 slice. The times are simulated.
32 devices in a mesh: groups: 2 (over y), tm: 4 (over x, core), win: 4 (over z).
Axes of the slice: x: 2, y: 2, z: 4, core: 2. Of those that a mesh axis runs over, the one named last changes fastest.
Arguments:
- unitaries: float32 [8, 4, 2, 2, 256, 256], P(('groups', 'win'), 'tm'), parts along dimension 0, may hold values from -1 to 1, as said below
Outputs:
- propagators: float32 [8, 4, 2, 2, 256, 256], P(('groups', 'win'), 'tm'), parts along dimension 0
There are 2 independent parts, one for each index of `groups`. A program takes and returns all parts, laid end to end along the dimension named above; each array names one. Nothing has to cross between parts.
Inputs may be any that keep to these rules, and one draw needn't show every extreme that they name: `unitaries`: each slot's complex matrix is unitary.
All inputs are finite; a program needn't handle non-finite values.
Results may differ from a plain program's by a relative error of at most 0.0003.
Values sent between devices are 32-bit elements; how exact they have to be, the bound alone decides.
A program may use at most 64 MiB of HBM per device.

v0:
```python
import jax
import jax.numpy as jnp
from jax import lax
from jax.sharding import PartitionSpec as P


def prefix(value, axis, join, neutral):
    count, mine = (lax.axis_size(axis), lax.axis_index(axis))
    pieces = lax.all_gather(value, axis)
    running = jnp.full_like(value, 0) + jnp.asarray(neutral, value.dtype)

    def hop(position, running):
        longer = join(running, pieces[position])
        return jnp.where(position < mine, longer, running)

    return lax.fori_loop(0, count - 1, hop, running)


def from_root(value, axis, source):
    kept = jnp.where(lax.axis_index(axis) == source, value, 0).astype(value.dtype)
    return lax.psum(kept, axis)


def complex_product(left, right):
    hi = lax.Precision.HIGHEST
    real_part = jnp.dot(
        left[0], right[0], precision=hi, preferred_element_type=jnp.float32
    ) - jnp.dot(left[1], right[1], precision=hi, preferred_element_type=jnp.float32)
    imag_part = jnp.dot(
        left[0], right[1], precision=hi, preferred_element_type=jnp.float32
    ) + jnp.dot(left[1], right[0], precision=hi, preferred_element_type=jnp.float32)
    return jnp.stack([real_part, imag_part])


def later_first(earlier, later):
    return complex_product(later, earlier)


def on_device(unitaries):
    own_slots = unitaries[0, 0]
    width = own_slots.shape[-1]
    identity_pair = jnp.stack(
        [jnp.eye(width, dtype=jnp.float32), jnp.zeros((width, width), jnp.float32)]
    )
    prefixes = [own_slots[0]]
    prefixes.append(complex_product(own_slots[1], prefixes[-1]))
    block_total = prefixes[-1]
    before = prefix(block_total, "tm", later_first, identity_pair)
    through = complex_product(block_total, before)
    window_product = from_root(through, "tm", lax.axis_size("tm") - 1)
    window_carry = prefix(window_product, "win", later_first, identity_pair)
    offset = complex_product(before, window_carry)
    results = jnp.stack([complex_product(piece, offset) for piece in prefixes])
    return results[None, None]


def solution(mesh):
    placed = (P(("groups", "win"), "tm", None, None, None, None),)
    return jax.shard_map(
        on_device,
        mesh=mesh,
        in_specs=placed,
        out_specs=P(("groups", "win"), "tm", None, None, None, None),
        check_vma=False,
    )
```

profile of v0, /device:TPU:0, one launch (start us, length us, event | category | flops | bytes accessed | tf_op | source)
XLA Modules:
  0.0 168.4 jit_solution(17108181392384072371)
XLA Ops:
  6.5 1.5 fusion.67
  8.0 1.4 fusion.57
  9.5 1.4 convolution_subtract_fusion.6
  10.9 0.4 convolution_add_fusion.6
  11.3 0.8 pad_maximum_fusion
  12.1 0.0 all-gather.6.cloned.1.call-update
  12.1 0.0 all-reduce.3.cloned.1.call-start
  12.3 25.3 %all-gather.6.cloned.1.call-done = f32[8,256,256]{2,1,0:T(8,128)} async-done(((f32[2,256,256]{2,1,0:T(8,128)}), f32[8,256,256]{2,1,0:T(8,128)}) %all-gather.6.cloned.1.call-update) | async-done | bytes 2097168 | tf_op jit(solution)/shard_map/all_gather | solution.py:9
  37.6 16.6 %while.26 = (s32[]{:T(128)}, f32[2,256,256]{2,1,0:T(8,128)S(1)}, s32[]{:T(128)}, f32[4,2,256,256]{3,2,1,0:T(8,128)}, s32[]{:T(128)}, /*index=5*/s32[]{:T(128)}, s32[]{}) while((s32[]{:T(128)}, f32[2,256,256]{2,1,0:T(8,128)S(1)}, s32[]{:T(128)}, f32[4,2,256,256]{3,2,1,0:T(8,128)}, s32[]{:T(128)}, /*index=5*/s32[]{:T(128)}, s32[]{}) %tuple.64), condition=%wide.region_1.2_spmd, body=%wide.region_0.1_spmd.sunk | while | flops 805699584 | bytes 5245035 | solution.py:16
  37.6 1.3 fusion.133
  38.9 1.3 fusion.134
  40.2 1.3 fusion.135
  41.6 1.3 fusion.136
  42.9 0.1 maximum_select_fusion.5
  43.1 1.3 fusion.133
  44.4 1.3 fusion.134
  45.8 1.3 fusion.135
  47.1 1.3 fusion.136
  48.5 0.1 maximum_select_fusion.5
  48.6 1.3 fusion.133
  49.9 1.3 fusion.134
  51.3 1.3 fusion.135
  52.6 1.3 fusion.136
  54.0 0.1 maximum_select_fusion.5
  54.1 0.4 fusion.53
  54.5 0.4 fusion.47
  54.9 0.4 fusion.37
  55.3 0.4 fusion.36
  55.7 0.8 fusion.38
  56.5 0.0 all-reduce.3.cloned.1.call-update
  56.5 0.2 all-gather.4.cloned.1.call-start
  56.8 33.1 %all-reduce.3.cloned.1.call-done = f32[1,2,256,256]{3,2,1,0:T(8,128)} async-done(((f32[1,2,256,256]{3,2,1,0:T(8,128)}), f32[1,2,256,256]{3,2,1,0:T(8,128)}) %all-reduce.3.cloned.1.call-update) | async-done | bytes 524304 | tf_op jit(solution)/shard_map/psum | solution.py:21
  89.9 47.5 %all-gather.4.cloned.1.call-done = f32[4,2,256,256]{3,2,1,0:T(8,128)} async-done(((f32[1,2,256,256]{3,2,1,0:T(8,128)}), f32[4,2,256,256]{3,2,1,0:T(8,128)}) %all-gather.4.cloned.1.call-update) | async-done | bytes 2097168 | tf_op jit(solution)/shard_map/all_gather | solution.py:9
  137.4 16.6 %while.27 = (s32[]{:T(128)}, f32[2,256,256]{2,1,0:T(8,128)S(1)}, s32[]{:T(128)}, f32[4,2,256,256]{3,2,1,0:T(8,128)}, s32[]{:T(128)}, /*index=5*/s32[]{:T(128)}, s32[]{}) while((s32[]{:T(128)}, f32[2,256,256]{2,1,0:T(8,128)S(1)}, s32[]{:T(128)}, f32[4,2,256,256]{3,2,1,0:T(8,128)}, s32[]{:T(128)}, /*index=5*/s32[]{:T(128)}, s32[]{}) %tuple.55), condition=%wide.region_4.5_spmd, body=%wide.region_3.4_spmd.sunk | while | flops 805699584 | bytes 5245035 | solution.py:16
  137.4 1.3 fusion.141
  138.8 1.3 fusion.142
  140.1 1.3 fusion.143
  141.4 1.3 fusion.144
  142.8 0.1 maximum_select_fusion.6
  142.9 1.3 fusion.141
  144.3 1.3 fusion.142
  145.6 1.3 fusion.143
  147.0 1.3 fusion.144
  148.3 0.1 maximum_select_fusion.6
  148.5 1.3 fusion.141
  149.8 1.3 fusion.142
  151.1 1.3 fusion.143
  152.5 1.3 fusion.144
  153.8 0.1 maximum_select_fusion.6
  154.0 0.4 fusion.43
  154.4 0.4 fusion.39
  154.8 0.4 convolution_subtract_fusion.4
  155.2 0.6 fusion.95
  155.8 0.6 fusion.64
  156.4 0.4 convolution_add_fusion.4
  156.7 0.6 fusion.96
  157.4 0.6 fusion.62
  158.0 0.6 fusion.33
  158.6 0.6 fusion.32
  159.2 0.6 fusion.35
  159.8 0.6 fusion.34
  160.4 0.1 maximum_bitcast_fusion.1
  160.5 0.1 maximum_bitcast_fusion
  160.6 1.3 copy.11
  (7 shorter events, 0.1 us)
Async XLA Ops:
  6.5 4.3 %copy-start = (f32[1,1,2,2,256,256]{5,4,3,2,1,0:T(8,128)S(1)}, f32[1,1,2,2,256,256]{5,4,3,2,1,0:T(8,128)}, u32[]{:S(2)}) copy-start(f32[1,1,2,2,256,256]{5,4,3,2,1,0:T(8,128)} %param.5) | copy-start | bytes 3145732
  6.5 31.0 %all-gather.6.cloned.1.call-start = ((), (), s32[]{:S(2)}) async-start(), calls=%async_computation.2 | async-start | bytes 2621440 | tf_op jit(solution)/shard_map/all_gather | solution.py:9
  12.1 77.7 %all-reduce.3.cloned.1.call-start = ((), (), s32[]{:S(2)}) async-start(), calls=%async_computation | async-start | bytes 1048576 | tf_op jit(solution)/shard_map/psum | solution.py:21
  56.5 80.9 %all-gather.4.cloned.1.call-start = ((), (), s32[]{:S(2)}) async-start(), calls=%async_computation.1 | async-start | bytes 2621440 | tf_op jit(solution)/shard_map/all_gather | solution.py:9
Sparse Core Ops, SparseCore 0:
  12.3 25.2 all-gather.5
  56.7 33.1 all-reduce.2
  91.4 45.9 all-gather.3
where the time goes:
time: 169 us; the launch traced here: 168 us
  waiting for transfers between devices  106 us (63%)
  matrix products  44.5 us (26%)
  between operations  13.3 us (8%)
  other arithmetic  2.66 us (2%)
    all_gather x2, waiting for transfers between devices, prefix(): pieces = lax.all_gather(value, axis)  72.8 us
    psum x1, waiting for transfers between devices, from_root(): return lax.psum(kept, axis)  33.1 us
    dot_general x11, matrix products, complex_product(): jnp.dot(left[0], right[0], precision=hi, preferred_element_type=jnp.float32)  11.5 us
    dot_general x11, matrix products, complex_product(): jnp.dot(left[1], right[1], precision=hi, preferred_element_type=jnp.float32)  11.4 us
    dot_general x11, matrix products, complex_product(): jnp.dot(left[0], right[1], precision=hi, preferred_element_type=jnp.float32)  11.3 us
    dot_general x11, matrix products, complex_product(): jnp.dot(left[1], right[0], precision=hi, preferred_element_type=jnp.float32)  10.4 us
  transfers between devices with their start and end apart: 3, of which 3 were waited for; matrix products, arithmetic and copies ran while one was open for 0% of the time, Pallas kernels for 0%

commit v1 on v0

v1 whole, which is shorter than its diff:
```python
import functools
import jax
import jax.numpy as jnp
from jax import lax
from jax.sharding import PartitionSpec as P
from jax.experimental import pallas as pl
from jax.experimental.pallas import tpu as pltpu

F32 = jnp.float32
BF16 = jnp.bfloat16
MESH = pl.DeviceIdType.MESH
CHUNKS = 2


def split(a):
    hi = a.astype(BF16)
    return hi, (a - hi.astype(F32)).astype(BF16)


def real_dot(a, b, dims):
    def dot(p, q):
        return lax.dot_general(p, q, (dims, ((), ())), preferred_element_type=F32)

    return dot(a[0], b[0]) + (dot(a[0], b[1]) + dot(a[1], b[0]))


def product(a, b, transposed=False):
    dims = ((1,), (1,)) if transposed else ((1,), (0,))
    ar, ai = split(a[0]), split(a[1])
    br, bi = split(b[0]), split(b[1])
    real = real_dot(ar, br, dims) - real_dot(ai, bi, dims)
    imag = real_dot(ar, bi, dims) + real_dot(ai, br, dims)
    return real, imag


def pair(ref):
    return ref[0], ref[1]


def put(ref, value):
    ref[0] = value[0]
    ref[1] = value[1]


def kernel(
    tm, windows, u, out,
    total, sib, chips, win, first, second, carry, nxt,
    t_send, t_recv, c_send, c_recv, f_send, f_recv,
    z_send, z_recv, e_send, e_recv, g_send, g_recv,
):
    d = lax.axis_index("tm")
    z = lax.axis_index("win")
    x, c = d // 2, d % 2
    nx = tm // 2
    width = u.shape[-1]
    half = width // 2
    rows = width // tm
    step = rows // CHUNKS
    mate = {"tm": x * 2 + (1 - c)}

    barrier = pltpu.get_barrier_semaphore()

    def greet(to):
        pl.semaphore_signal(barrier, inc=1, device_id=to, device_id_type=MESH)

    greet(mate)
    for o in range(1, nx):
        greet({"tm": ((x + o) % nx) * 2 + c})

    @pl.when(z > 0)
    def _():
        greet({"win": z - 1})

    @pl.when(z < windows - 1)
    def _():
        greet({"win": z + 1})

    put(total, product(pair(u.at[1]), pair(u.at[0])))
    inner = (z > 0) & (z < windows - 1)

    @pl.when(inner)
    def _():
        pl.semaphore_wait(barrier, nx + 2)

    @pl.when(jnp.logical_not(inner))
    def _():
        pl.semaphore_wait(barrier, nx + 1)

    def copy(src, dst, send, recv, to):
        return pltpu.make_async_remote_copy(
            src_ref=src, dst_ref=dst, send_sem=send, recv_sem=recv,
            device_id=to, device_id_type=MESH,
        )

    t_copy = copy(total, sib, t_send, t_recv, mate)
    t_copy.start()
    t_copy.wait_recv()

    @pl.when(c == 0)
    def _():
        put(chips.at[x], product(pair(sib), pair(total)))

    @pl.when(c == 1)
    def _():
        put(chips.at[x], product(pair(total), pair(sib)))

    own_half = pl.ds(pl.multiple_of(c * half, half), half)
    other_half = pl.ds(pl.multiple_of((1 - c) * half, half), half)

    def c_copy(j, to):
        ref = chips.at[j, :, own_half, :]
        return copy(ref, ref, c_send.at[to], c_recv.at[j], {"tm": to * 2 + c})

    def f_copy(j, part):
        ref = chips.at[j, :, part, :]
        return copy(ref, ref, f_send.at[j], f_recv.at[j], mate)

    others = [(x + o) % nx for o in range(1, nx)]
    for j in others:
        c_copy(x, j).start()

    @pl.when(c == 0)
    def _():
        put(first, pair(u.at[0]))
        put(second, pair(total))

    @pl.when(c == 1)
    def _():
        put(first, product(pair(u.at[0]), pair(sib)))
        put(second, pair(chips.at[x]))

    for j in others:
        c_copy(j, x).wait_recv()
        f_copy(j, own_half).start()
    for j in others:
        f_copy(j, other_half).wait_recv()

    put(win, pair(chips.at[0]))

    def apply_before():
        before = pair(win)
        put(first, product(pair(first), before))
        put(second, product(pair(second), before))

    def join(j, _):
        @pl.when((j == x) & (z > 0))
        def _():
            apply_before()

        put(win, product(pair(chips.at[j]), pair(win)))
        return 0

    if nx == 2:
        @pl.when((x == 1) & (z > 0))
        def _():
            apply_before()

        put(win, product(pair(chips.at[1]), pair(win)))
    else:
        lax.fori_loop(1, nx, join, 0)

    def piece(owner, k):
        return pl.ds(pl.multiple_of(owner * rows + k * step, step), step)

    def z_copy(k):
        return copy(
            nxt.at[k], carry.at[:, piece(d, k), :], z_send.at[k], z_recv.at[k], {"win": z + 1}
        )

    def advance(k, held):
        put(nxt.at[k], product(held, pair(win), transposed=True))
        z_copy(k).start()

    def e_copy(j, to, k):
        ref = carry.at[:, piece(j * 2 + c, k), :]
        return copy(ref, ref, e_send.at[to, k], e_recv.at[j, k], {"tm": to * 2 + c})

    def g_copy(j, core, k):
        ref = carry.at[:, piece(j * 2 + core, k), :]
        return copy(ref, ref, g_send.at[j, k], g_recv.at[j, k], mate)

    @pl.when(z == 0)
    def _():
        for k in range(CHUNKS):
            row = lax.broadcasted_iota(jnp.int32, (step, width), 0) + (d * rows + k * step)
            column = lax.broadcasted_iota(jnp.int32, (step, width), 1)
            advance(k, ((row == column).astype(F32), jnp.zeros((step, width), F32)))

        if nx > 2:
            put(win, pair(chips.at[0]))

            def redo(j, _):
                @pl.when(j == x)
                def _():
                    apply_before()

                put(win, product(pair(chips.at[j]), pair(win)))
                return 0

            lax.fori_loop(1, nx, redo, 0)
        else:
            put(win, pair(chips.at[0]))

            @pl.when(x == 1)
            def _():
                apply_before()

        put(out.at[0], pair(first))
        put(out.at[1], pair(second))

    @pl.when(z > 0)
    def _():
        for k in range(CHUNKS):
            ref = carry.at[:, piece(d, k), :]
            copy(nxt.at[k], ref, z_send.at[k], z_recv.at[k], {"win": z - 1}).wait_recv()
            for j in others:
                e_copy(x, j, k).start()
            g_copy(x, c, k).start()

            @pl.when(z < windows - 1)
            def _():
                advance(k, pair(ref))

        for k in range(CHUNKS):
            for j in others:
                e_copy(j, x, k).wait_recv()
                g_copy(j, c, k).start()
        for k in range(CHUNKS):
            g_copy(x, 1 - c, k).wait_recv()
            for j in others:
                g_copy(j, 1 - c, k).wait_recv()
        before = pair(carry)
        put(out.at[0], product(pair(first), before, transposed=True))
        put(out.at[1], product(pair(second), before, transposed=True))
        for k in range(CHUNKS):
            for j in others:
                e_copy(x, j, k).wait_send()
                g_copy(j, c, k).wait_send()
            g_copy(x, c, k).wait_send()

    @pl.when(z < windows - 1)
    def _():
        for k in range(CHUNKS):
            z_copy(k).wait_send()

    t_copy.wait_send()
    for j in others:
        c_copy(x, j).wait_send()
        f_copy(j, own_half).wait_send()


def on_device(tm, windows, unitaries):
    u = unitaries[0, 0]
    width = u.shape[-1]
    nx = tm // 2
    dma = pltpu.SemaphoreType.DMA
    mat = pltpu.VMEM((2, width, width), F32)
    step = width // tm // CHUNKS
    result = pl.pallas_call(
        functools.partial(kernel, tm, windows),
        out_shape=jax.ShapeDtypeStruct(u.shape, F32),
        in_specs=[pl.BlockSpec(memory_space=pltpu.VMEM)],
        out_specs=pl.BlockSpec(memory_space=pltpu.VMEM),
        scratch_shapes=[
            mat, mat, pltpu.VMEM((nx, 2, width, width), F32), mat, mat, mat, mat,
            pltpu.VMEM((CHUNKS, 2, step, width), F32),
            dma, dma, dma((nx,)), dma((nx,)), dma((nx,)), dma((nx,)),
            dma((CHUNKS,)), dma((CHUNKS,)),
            dma((nx, CHUNKS)), dma((nx, CHUNKS)), dma((nx, CHUNKS)), dma((nx, CHUNKS)),
        ],
        compiler_params=pltpu.CompilerParams(
            collective_id=0, has_side_effects=True, vmem_limit_bytes=40 * 1024 * 1024
        ),
    )(u)
    return result[None, None]


def solution(mesh):
    placed = P(("groups", "win"), "tm", None, None, None, None)
    return jax.shard_map(
        functools.partial(on_device, mesh.shape["tm"], mesh.shape["win"]),
        mesh=mesh,
        in_specs=(placed,),
        out_specs=placed,
        check_vma=False,
    )
```

time: 169 us -> 33.4 us (0.20)
  the two profiles are of different devices: /device:TPU:0 before, /device:TPU:25 now
where the time goes in v1:
time: 33.4 us; the launch traced here: 33.2 us
  Pallas kernels  31 us (93%)
  local copies, waits for them, and re-layouts  2.2 us (7%)
    pallas_call x1, Pallas kernels, on_device(): pl.pallas_call(functools.partial(kernel, tm, windows), out_shape=jax.Shap...  31 us
    unnamed x3, local copies, waits for them, and re-layouts  2.2 us

profile of v1, /device:TPU:25, one launch (start us, length us, event | category | flops | bytes accessed | tf_op | source)
XLA Modules:
  0.0 33.2 jit_solution(10135341859209088458)
XLA Ops:
  0.0 0.0 copy-start
  0.0 1.2 %copy-done = f32[1,1,2,2,256,256]{5,4,3,2,1,0:T(8,128)S(1)} copy-done((f32[1,1,2,2,256,256]{5,4,3,2,1,0:T(8,128)S(1)}, f32[1,1,2,2,256,256]{5,4,3,2,1,0:T(8,128)}, u32[]{:S(2)}) %copy-start) | copy-done | bytes 1048600
  1.2 31.0 %shard_map.17 = f32[2,2,256,256]{3,2,1,0:T(8,128)S(1)} custom-call(f32[2,2,256,256]{3,2,1,0:T(8,128)S(1)} %bitcast.3), custom_call_target="tpu_custom_call" | custom-call | tf_op jit(solution)/shard_map/pallas_call | solution.py:259
  32.3 1.0 %copy.3 = f32[1,1,2,2,256,256]{5,4,3,2,1,0:T(8,128)} copy(f32[1,1,2,2,256,256]{5,4,3,2,1,0:T(8,128)S(1)} %bitcast.2) | data formatting | bytes 2097152
Async XLA Ops:
  0.0 1.2 %copy-start = (f32[1,1,2,2,256,256]{5,4,3,2,1,0:T(8,128)S(1)}, f32[1,1,2,2,256,256]{5,4,3,2,1,0:T(8,128)}, u32[]{:S(2)}) copy-start(f32[1,1,2,2,256,256]{5,4,3,2,1,0:T(8,128)} %param.1) | copy-start | bytes 3145732

commit v2 on v1

v2 whole, which is shorter than its diff:
```python
import functools
import jax
import jax.numpy as jnp
from jax import lax
from jax.sharding import PartitionSpec as P
from jax.experimental import pallas as pl
from jax.experimental.pallas import tpu as pltpu

F32 = jnp.float32
BF16 = jnp.bfloat16
MESH = pl.DeviceIdType.MESH
CHUNKS = 2
PIECES = 2
NT = (((1,), (1,)), ((), ()))
NN = (((1,), (0,)), ((), ()))


def split(a):
    hi = a.astype(BF16)
    return hi, (a - hi.astype(F32)).astype(BF16)


def real_dot(a, b, dims):
    def dot(p, q):
        return lax.dot_general(p, q, dims, preferred_element_type=F32)

    return dot(a[0], b[0]) + (dot(a[0], b[1]) + dot(a[1], b[0]))


def product(a, b, transposed=False):
    dims = NT if transposed else NN
    ar, ai = split(a[0]), split(a[1])
    br, bi = split(b[0]), split(b[1])
    real = real_dot(ar, br, dims) - real_dot(ai, bi, dims)
    imag = real_dot(ar, bi, dims) + real_dot(ai, br, dims)
    return real, imag


def put_split(ref, value):
    ref[0], ref[1] = split(value[0])
    ref[2], ref[3] = split(value[1])


def row_product(a, w):
    m = a[0].shape[0]
    (rh, rl), (ih, il) = split(a[0]), split(a[1])
    stack = jnp.concatenate([rh, ih, rl, il], axis=0)
    top = jnp.concatenate([rh, ih], axis=0)

    def dot(p, q):
        return lax.dot_general(p, q, NT, preferred_element_type=F32)

    by_real = dot(stack, w[0])
    by_real = by_real[: 2 * m] + by_real[2 * m :] + dot(top, w[1])
    by_imag = dot(stack, w[2])
    by_imag = by_imag[: 2 * m] + by_imag[2 * m :] + dot(top, w[3])
    return by_real[:m] - by_imag[m:], by_real[m:] + by_imag[:m]


def pair(ref):
    return ref[0], ref[1]


def put(ref, value):
    ref[0] = value[0]
    ref[1] = value[1]


def kernel(
    tm, windows, u_hbm, out,
    u, total, sib, chips, win, first, second, carry, nxt, wsp,
    u_sem, t_send, t_recv, c_send, c_recv, f_send, f_recv,
    s_send, s_recv, z_send, z_recv, e_send, e_recv, g_send, g_recv,
):
    d = lax.axis_index("tm")
    z = lax.axis_index("win")
    x, c = d // 2, d % 2
    nx = tm // 2
    direct = nx == 2
    width = u.shape[-1]
    half = width // 2
    rows = width // tm
    step = rows // CHUNKS
    part = half // PIECES
    mate = {"tm": x * 2 + (1 - c)}
    last = windows - 1

    loads = [pltpu.make_async_copy(u_hbm.at[s], u.at[s], u_sem.at[s]) for s in range(2)]
    for load in loads:
        load.start()

    barrier = pltpu.get_barrier_semaphore()

    def greet(to):
        pl.semaphore_signal(barrier, inc=1, device_id=to, device_id_type=MESH)

    greet(mate)
    for o in range(1, nx):
        greet({"tm": ((x + o) % nx) * 2 + c})

    if direct:
        @pl.when(z > 1)
        def _():
            greet({"win": z - 1})

        @pl.when(z == 1)
        def _():
            greet({"win": 0, "tm": 2 + c})

        @pl.when((z == 0) & (x == 1))
        def _():
            greet({"win": 1, "tm": c})
            greet({"win": 1, "tm": 2 + c})

        @pl.when((z > 0) & (z < last))
        def _():
            greet({"win": z + 1})
    else:
        @pl.when(z > 0)
        def _():
            greet({"win": z - 1})

        @pl.when(z < last)
        def _():
            greet({"win": z + 1})

    for load in loads:
        load.wait()
    put(total, product(pair(u.at[1]), pair(u.at[0])))

    inner = (z > 0) & (z < last)
    if direct:
        start = (z == 0) & (x == 0)
        many = inner | ((z == 0) & (x == 1))

        @pl.when(start)
        def _():
            pl.semaphore_wait(barrier, nx)

        @pl.when(many)
        def _():
            pl.semaphore_wait(barrier, nx + 2)

        @pl.when(z == last)
        def _():
            pl.semaphore_wait(barrier, nx + 1)
    else:
        @pl.when(inner)
        def _():
            pl.semaphore_wait(barrier, nx + 2)

        @pl.when(jnp.logical_not(inner))
        def _():
            pl.semaphore_wait(barrier, nx + 1)

    def copy(src, dst, send, recv, to):
        return pltpu.make_async_remote_copy(
            src_ref=src, dst_ref=dst, send_sem=send, recv_sem=recv,
            device_id=to, device_id_type=MESH,
        )

    t_copy = copy(total, sib, t_send, t_recv, mate)
    t_copy.start()
    t_copy.wait_recv()

    @pl.when(c == 0)
    def _():
        put(chips.at[x], product(pair(sib), pair(total)))

    @pl.when(c == 1)
    def _():
        put(chips.at[x], product(pair(total), pair(sib)))

    others = [(x + o) % nx for o in range(1, nx)]

    def local():
        @pl.when(c == 0)
        def _():
            put(first, pair(u.at[0]))
            put(second, pair(total))

        @pl.when(c == 1)
        def _():
            put(first, product(pair(u.at[0]), pair(sib)))
            put(second, pair(chips.at[x]))

    def band(core, q):
        return pl.ds(pl.multiple_of(core * half + q * part, part), part)

    def c_copy(j, to, q):
        ref = chips.at[j, :, band(c, q), :]
        return copy(ref, ref, c_send.at[to, q], c_recv.at[j, q], {"tm": to * 2 + c})

    def f_copy(j, core, q):
        ref = chips.at[j, :, band(core, q), :]
        return copy(ref, ref, f_send.at[j, q], f_recv.at[j, q], mate)

    def exchange():
        for q in range(PIECES):
            for j in others:
                c_copy(x, j, q).start()
        local()
        for q in range(PIECES):
            for j in others:
                c_copy(j, x, q).wait_recv()
                f_copy(j, c, q).start()
        for q in range(PIECES):
            for j in others:
                f_copy(j, 1 - c, q).wait_recv()

    def exchange_sent():
        for q in range(PIECES):
            for j in others:
                c_copy(x, j, q).wait_send()
                f_copy(j, c, q).wait_send()

    def apply_before(before):
        put(first, product(pair(first), before))
        put(second, product(pair(second), before))

    def whole_window():
        if direct:
            put(win, product(pair(chips.at[1]), pair(chips.at[0])))
        else:
            put(win, pair(chips.at[0]))

            def join(j, _):
                put(win, product(pair(chips.at[j]), pair(win)))
                return 0

            lax.fori_loop(1, nx, join, 0)
        put_split(wsp, pair(win))

    def chips_before():
        @pl.when(x > 0)
        def _():
            if not direct:
                put(win, pair(chips.at[0]))

                def join(j, _):
                    put(win, product(pair(chips.at[j]), pair(win)))
                    return 0

                lax.fori_loop(1, x, join, 0)
                apply_before(pair(win))
            else:
                apply_before(pair(chips.at[0]))

    def piece(owner, k):
        return pl.ds(pl.multiple_of(owner * rows + k * step, step), step)

    def identity_rows(owner, k):
        row = lax.broadcasted_iota(jnp.int32, (step, width), 0) + (owner * rows + k * step)
        column = lax.broadcasted_iota(jnp.int32, (step, width), 1)
        return (row == column).astype(F32)

    def z_copy(k, to):
        return copy(
            nxt.at[k, :, pl.ds(0, step), :], carry.at[:, piece(d, k), :],
            z_send.at[k, 0], z_recv.at[k], {"win": to},
        )

    def e_copy(j, to, k):
        ref = carry.at[:, piece(j * 2 + c, k), :]
        return copy(ref, ref, e_send.at[to, k], e_recv.at[j, k], {"tm": to * 2 + c})

    def g_copy(j, core, k):
        ref = carry.at[:, piece(j * 2 + core, k), :]
        return copy(ref, ref, g_send.at[j, k], g_recv.at[j, k], mate)

    def finish():
        before = pair(carry)
        put(out.at[0], product(pair(first), before, transposed=True))
        put(out.at[1], product(pair(second), before, transposed=True))

    def finish_first():
        put(out.at[0], pair(first))
        put(out.at[1], pair(second))

    if direct:
        def s_copy(k, i):
            return copy(
                nxt.at[k, :, pl.ds(i * step, step), :], carry.at[:, piece(2 * i + c, k), :],
                s_send.at[k, i], s_recv.at[k, i], {"tm": 2 + c},
            )

        def o_copy(k, i):
            return copy(
                nxt.at[k, :, pl.ds(i * step, step), :], carry.at[:, piece(2 * i + c, k), :],
                z_send.at[k, i], z_recv.at[k], {"win": 1, "tm": 2 * i + c},
            )

        @pl.when((z == 0) & (x == 0))
        def _():
            put_split(wsp, pair(chips.at[0]))
            for k in range(CHUNKS):
                real = jnp.concatenate([identity_rows(c, k), identity_rows(2 + c, k)], axis=0)
                put(nxt.at[k], row_product((real, jnp.zeros_like(real)), wsp))
                for i in range(2):
                    s_copy(k, i).start()
            local()
            finish_first()
            for k in range(CHUNKS):
                for i in range(2):
                    s_copy(k, i).wait_send()

        @pl.when((z == 0) & (x == 1))
        def _():
            put_split(wsp, pair(chips.at[1]))
            for k in range(CHUNKS):
                for i in range(2):
                    s_copy(k, i).wait_recv()
                    g_copy(i, c, k).start()
                held = [
                    jnp.concatenate([carry[p, piece(c, k), :], carry[p, piece(2 + c, k), :]], axis=0)
                    for p in range(2)
                ]
                put(nxt.at[k], row_product(held, wsp))
                for i in range(2):
                    o_copy(k, i).start()
            local()
            for k in range(CHUNKS):
                for i in range(2):
                    g_copy(i, 1 - c, k).wait_recv()
            finish()
            for k in range(CHUNKS):
                for i in range(2):
                    g_copy(i, c, k).wait_send()
                    o_copy(k, i).wait_send()
    else:
        @pl.when(z == 0)
        def _():
            exchange()
            whole_window()
            for k in range(CHUNKS):
                real = identity_rows(d, k)
                put(nxt.at[k, :, pl.ds(0, step), :], row_product((real, jnp.zeros_like(real)), wsp))
                z_copy(k, 1).start()
            chips_before()
            finish_first()
            for k in range(CHUNKS):
                z_copy(k, 1).wait_send()
            exchange_sent()

    @pl.when(z > 0)
    def _():
        exchange()

        @pl.when(z < last)
        def _():
            whole_window()

        @pl.when(z > 1)
        def _():
            chips_before()

        for k in range(CHUNKS):
            ref = carry.at[:, piece(d, k), :]
            z_copy(k, z).wait_recv()
            for j in others:
                e_copy(x, j, k).start()
            g_copy(x, c, k).start()

            @pl.when(z < last)
            def _():
                put(nxt.at[k, :, pl.ds(0, step), :], row_product(pair(ref), wsp))
                z_copy(k, z + 1).start()

        for k in range(CHUNKS):
            for j in others:
                e_copy(j, x, k).wait_recv()
                g_copy(j, c, k).start()

        @pl.when(z == 1)
        def _():
            chips_before()

        for k in range(CHUNKS):
            g_copy(x, 1 - c, k).wait_recv()
            for j in others:
                g_copy(j, 1 - c, k).wait_recv()
        finish()
        for k in range(CHUNKS):
            for j in others:
                e_copy(x, j, k).wait_send()
                g_copy(j, c, k).wait_send()
            g_copy(x, c, k).wait_send()

        @pl.when(z < last)
        def _():
            for k in range(CHUNKS):
                z_copy(k, z + 1).wait_send()

        exchange_sent()

    t_copy.wait_send()


def on_device(tm, windows, unitaries):
    u = unitaries[0, 0]
    width = u.shape[-1]
    nx = tm // 2
    dma = pltpu.SemaphoreType.DMA
    mat = pltpu.VMEM((2, width, width), F32)
    step = width // tm // CHUNKS
    result = pl.pallas_call(
        functools.partial(kernel, tm, windows),
        out_shape=jax.ShapeDtypeStruct(u.shape, F32),
        in_specs=[pl.BlockSpec(memory_space=pl.ANY)],
        out_specs=pl.BlockSpec(memory_space=pltpu.VMEM),
        scratch_shapes=[
            pltpu.VMEM((2, 2, width, width), F32),
            mat, mat, pltpu.VMEM((nx, 2, width, width), F32), mat, mat, mat, mat,
            pltpu.VMEM((CHUNKS, 2, 2 * step, width), F32),
            pltpu.VMEM((4, width, width), BF16),
            dma((2,)), dma, dma,
            dma((nx, PIECES)), dma((nx, PIECES)), dma((nx, PIECES)), dma((nx, PIECES)),
            dma((CHUNKS, 2)), dma((CHUNKS, 2)), dma((CHUNKS, 2)), dma((CHUNKS,)),
            dma((nx, CHUNKS)), dma((nx, CHUNKS)), dma((nx, CHUNKS)), dma((nx, CHUNKS)),
        ],
        compiler_params=pltpu.CompilerParams(
            collective_id=0, has_side_effects=True, vmem_limit_bytes=40 * 1024 * 1024
        ),
    )(u)
    return result[None, None]


def solution(mesh):
    placed = P(("groups", "win"), "tm", None, None, None, None)
    return jax.shard_map(
        functools.partial(on_device, mesh.shape["tm"], mesh.shape["win"]),
        mesh=mesh,
        in_specs=(placed,),
        out_specs=placed,
        check_vma=False,
    )
```

time: 33.4 us -> 31.2 us (0.934)
  Pallas kernels: 31 us -> 28.9 us
    pallas_call x1, Pallas kernels: 31 us -> 28.9 us  [on_device(): pl.pallas_call(functools.partial(kernel, tm, windows), out_shape=jax.Shap...]
where the time goes in v2:
time: 31.2 us; the launch traced here: 31.1 us
  Pallas kernels  28.9 us (93%)
  local copies, waits for them, and re-layouts  2.2 us (7%)
    pallas_call x1, Pallas kernels, on_device(): pl.pallas_call(functools.partial(kernel, tm, windows), out_shape=jax.Shap...  28.9 us
    unnamed x3, local copies, waits for them, and re-layouts  2.2 us

profile of v2, /device:TPU:25, one launch (start us, length us, event | category | flops | bytes accessed | tf_op | source)
XLA Modules:
  0.0 31.1 jit_solution(16954241816789701407)
XLA Ops:
  0.0 0.0 copy-start
  0.0 1.2 %copy-done = f32[1,1,2,2,256,256]{5,4,3,2,1,0:T(8,128)S(1)} copy-done((f32[1,1,2,2,256,256]{5,4,3,2,1,0:T(8,128)S(1)}, f32[1,1,2,2,256,256]{5,4,3,2,1,0:T(8,128)}, u32[]{:S(2)}) %copy-start) | copy-done | bytes 1048600
  1.2 28.9 %shard_map.17 = f32[2,2,256,256]{3,2,1,0:T(8,128)S(1)} custom-call(f32[2,2,256,256]{3,2,1,0:T(8,128)S(1)} %bitcast.3), custom_call_target="tpu_custom_call" | custom-call | tf_op jit(solution)/shard_map/pallas_call | solution.py:406
  30.1 1.0 %copy.3 = f32[1,1,2,2,256,256]{5,4,3,2,1,0:T(8,128)} copy(f32[1,1,2,2,256,256]{5,4,3,2,1,0:T(8,128)S(1)} %bitcast.2) | data formatting | bytes 2097152
Async XLA Ops:
  0.0 1.2 %copy-start = (f32[1,1,2,2,256,256]{5,4,3,2,1,0:T(8,128)S(1)}, f32[1,1,2,2,256,256]{5,4,3,2,1,0:T(8,128)}, u32[]{:S(2)}) copy-start(f32[1,1,2,2,256,256]{5,4,3,2,1,0:T(8,128)} %param.1) | copy-start | bytes 3145732

commit v3 on v2

--- a/solution.py
+++ b/solution.py
@@ -9,7 +9,8 @@
 F32 = jnp.float32
 BF16 = jnp.bfloat16
 MESH = pl.DeviceIdType.MESH
-CHUNKS = 2
+MOST_CHUNKS = 4
+LEAD = 4
 PIECES = 2
 NT = (((1,), (1,)), ((), ()))
 NN = (((1,), (0,)), ((), ()))
@@ -64,6 +65,10 @@
 def put(ref, value):
     ref[0] = value[0]
     ref[1] = value[1]
+
+
+def carry_chunks(rows):
+    return max(1, min(MOST_CHUNKS, rows // 8))
 
 
 def kernel(
@@ -80,7 +85,8 @@
     width = u.shape[-1]
     half = width // 2
     rows = width // tm
-    step = rows // CHUNKS
+    chunks = carry_chunks(rows)
+    step = rows // chunks
     part = half // PIECES
     mate = {"tm": x * 2 + (1 - c)}
     last = windows - 1
@@ -98,60 +104,26 @@
     for o in range(1, nx):
         greet({"tm": ((x + o) % nx) * 2 + c})
 
-    if direct:
-        @pl.when(z > 1)
-        def _():
-            greet({"win": z - 1})
-
-        @pl.when(z == 1)
-        def _():
-            greet({"win": 0, "tm": 2 + c})
-
-        @pl.when((z == 0) & (x == 1))
-        def _():
-            greet({"win": 1, "tm": c})
-            greet({"win": 1, "tm": 2 + c})
-
-        @pl.when((z > 0) & (z < last))
-        def _():
-            greet({"win": z + 1})
-    else:
-        @pl.when(z > 0)
-        def _():
-            greet({"win": z - 1})
-
-        @pl.when(z < last)
-        def _():
-            greet({"win": z + 1})
+    @pl.when(z > 0)
+    def _():
+        greet({"win": z - 1})
+
+    @pl.when(z < last)
+    def _():
+        greet({"win": z + 1})
 
     for load in loads:
         load.wait()
     put(total, product(pair(u.at[1]), pair(u.at[0])))
 
     inner = (z > 0) & (z < last)
-    if direct:
-        start = (z == 0) & (x == 0)
-        many = inner | ((z == 0) & (x == 1))
-
-        @pl.when(start)
-        def _():
-            pl.semaphore_wait(barrier, nx)
-
-        @pl.when(many)
-        def _():
-            pl.semaphore_wait(barrier, nx + 2)
-
-        @pl.when(z == last)
-        def _():
-            pl.semaphore_wait(barrier, nx + 1)
-    else:
-        @pl.when(inner)
-        def _():
-            pl.semaphore_wait(barrier, nx + 2)
-
-        @pl.when(jnp.logical_not(inner))
-        def _():
-            pl.semaphore_wait(barrier, nx + 1)
+    @pl.when(inner)
+    def _():
+        pl.semaphore_wait(barrier, nx + 2)
+
+    @pl.when(jnp.logical_not(inner))
+    def _():
+        pl.semaphore_wait(barrier, nx + 1)
 
     def copy(src, dst, send, recv, to):
         return pltpu.make_async_remote_copy(
@@ -256,7 +228,7 @@
 
     def z_copy(k, to):
         return copy(
-            nxt.at[k, :, pl.ds(0, step), :], carry.at[:, piece(d, k), :],
+            nxt.at[k, 0], carry.at[:, piece(d, k), :],
             z_send.at[k, 0], z_recv.at[k], {"win": to},
         )
 
@@ -278,67 +250,79 @@
         put(out.at[1], pair(second))
 
     if direct:
+        order = sorted(
+            [(k, i) for k in range(chunks) for i in range(2)], key=lambda ki: ki[0] + LEAD * ki[1]
+        )
+
         def s_copy(k, i):
             return copy(
-                nxt.at[k, :, pl.ds(i * step, step), :], carry.at[:, piece(2 * i + c, k), :],
+                nxt.at[k, i], carry.at[:, piece(2 * i + c, k), :],
                 s_send.at[k, i], s_recv.at[k, i], {"tm": 2 + c},
             )
 
-        def o_copy(k, i):
+        def back_copy(k):
             return copy(
-                nxt.at[k, :, pl.ds(i * step, step), :], carry.at[:, piece(2 * i + c, k), :],
-                z_send.at[k, i], z_recv.at[k], {"win": 1, "tm": 2 * i + c},
+                nxt.at[k, 0], carry.at[:, piece(c, k), :],
+                z_send.at[k, 0], e_recv.at[1, k], {"tm": c},
             )
 
+        def relay_copy(k):
+            ref = carry.at[:, piece(d, k), :]
+            return copy(ref, ref, z_send.at[k, 0], z_recv.at[k], {"win": 1})
+
+        def up_copy(k):
+            return copy(
+                nxt.at[k, 1], carry.at[:, piece(d, k), :],
+                z_send.at[k, 1], z_recv.at[k], {"win": 1},
+            )
+
         @pl.when((z == 0) & (x == 0))
         def _():
             put_split(wsp, pair(chips.at[0]))
-            for k in range(CHUNKS):
-                real = jnp.concatenate([identity_rows(c, k), identity_rows(2 + c, k)], axis=0)
-                put(nxt.at[k], row_product((real, jnp.zeros_like(real)), wsp))
-                for i in range(2):
-                    s_copy(k, i).start()
+            for k, i in order:
+                real = identity_rows(2 * i + c, k)
+                put(nxt.at[k, i], row_product((real, jnp.zeros_like(real)), wsp))
+                s_copy(k, i).start()
             local()
+            for k in range(chunks):
+                back_copy(k).wait_recv()
+                relay_copy(k).start()
             finish_first()
-            for k in range(CHUNKS):
+            for k in range(chunks):
+                relay_copy(k).wait_send()
+            for k in range(chunks):
                 for i in range(2):
                     s_copy(k, i).wait_send()
 
         @pl.when((z == 0) & (x == 1))
         def _():
             put_split(wsp, pair(chips.at[1]))
-            for k in range(CHUNKS):
-                for i in range(2):
-                    s_copy(k, i).wait_recv()
-                    g_copy(i, c, k).start()
-                held = [
-                    jnp.concatenate([carry[p, piece(c, k), :], carry[p, piece(2 + c, k), :]], axis=0)
-                    for p in range(2)
-                ]
-                put(nxt.at[k], row_product(held, wsp))
-                for i in range(2):
-                    o_copy(k, i).start()
+            for k, i in order:
+                s_copy(k, i).wait_recv()
+                g_copy(i, c, k).start()
+                put(nxt.at[k, i], row_product(pair(carry.at[:, piece(2 * i + c, k), :]), wsp))
+                (up_copy if i else back_copy)(k).start()
             local()
-            for k in range(CHUNKS):
+            for k in range(chunks):
                 for i in range(2):
                     g_copy(i, 1 - c, k).wait_recv()
             finish()
-            for k in range(CHUNKS):
+            for k in range(chunks):
                 for i in range(2):
                     g_copy(i, c, k).wait_send()
-                    o_copy(k, i).wait_send()
+                    (up_copy if i else back_copy)(k).wait_send()
     else:
         @pl.when(z == 0)
         def _():
             exchange()
             whole_window()
-            for k in range(CHUNKS):
+            for k in range(chunks):
                 real = identity_rows(d, k)
-                put(nxt.at[k, :, pl.ds(0, step), :], row_product((real, jnp.zeros_like(real)), wsp))
+                put(nxt.at[k, 0], row_product((real, jnp.zeros_like(real)), wsp))
                 z_copy(k, 1).start()
             chips_before()
             finish_first()
-            for k in range(CHUNKS):
+            for k in range(chunks):
                 z_copy(k, 1).wait_send()
             exchange_sent()
 
@@ -354,7 +338,7 @@
         def _():
             chips_before()
 
-        for k in range(CHUNKS):
+        for k in range(chunks):
             ref = carry.at[:, piece(d, k), :]
             z_copy(k, z).wait_recv()
             for j in others:
@@ -363,10 +347,10 @@
 
             @pl.when(z < last)
             def _():
-                put(nxt.at[k, :, pl.ds(0, step), :], row_product(pair(ref), wsp))
+                put(nxt.at[k, 0], row_product(pair(ref), wsp))
                 z_copy(k, z + 1).start()
 
-        for k in range(CHUNKS):
+        for k in range(chunks):
             for j in others:
                 e_copy(j, x, k).wait_recv()
                 g_copy(j, c, k).start()
@@ -375,12 +359,12 @@
         def _():
             chips_before()
 
-        for k in range(CHUNKS):
+        for k in range(chunks):
             g_copy(x, 1 - c, k).wait_recv()
             for j in others:
                 g_copy(j, 1 - c, k).wait_recv()
         finish()
-        for k in range(CHUNKS):
+        for k in range(chunks):
             for j in others:
                 e_copy(x, j, k).wait_send()
                 g_copy(j, c, k).wait_send()
@@ -388,7 +372,7 @@
 
         @pl.when(z < last)
         def _():
-            for k in range(CHUNKS):
+            for k in range(chunks):
                 z_copy(k, z + 1).wait_send()
 
         exchange_sent()
@@ -402,7 +386,8 @@
     nx = tm // 2
     dma = pltpu.SemaphoreType.DMA
     mat = pltpu.VMEM((2, width, width), F32)
-    step = width // tm // CHUNKS
+    chunks = carry_chunks(width // tm)
+    step = width // tm // chunks
     result = pl.pallas_call(
         functools.partial(kernel, tm, windows),
         out_shape=jax.ShapeDtypeStruct(u.shape, F32),
@@ -411,15 +396,15 @@
         scratch_shapes=[
             pltpu.VMEM((2, 2, width, width), F32),
             mat, mat, pltpu.VMEM((nx, 2, width, width), F32), mat, mat, mat, mat,
-            pltpu.VMEM((CHUNKS, 2, 2 * step, width), F32),
+            pltpu.VMEM((chunks, 2, 2, step, width), F32),
             pltpu.VMEM((4, width, width), BF16),
             dma((2,)), dma, dma,
             dma((nx, PIECES)), dma((nx, PIECES)), dma((nx, PIECES)), dma((nx, PIECES)),
-            dma((CHUNKS, 2)), dma((CHUNKS, 2)), dma((CHUNKS, 2)), dma((CHUNKS,)),
-            dma((nx, CHUNKS)), dma((nx, CHUNKS)), dma((nx, CHUNKS)), dma((nx, CHUNKS)),
+            dma((chunks, 2)), dma((chunks, 2)), dma((chunks, 2)), dma((chunks,)),
+            dma((nx, chunks)), dma((nx, chunks)), dma((nx, chunks)), dma((nx, chunks)),
         ],
         compiler_params=pltpu.CompilerParams(
-            collective_id=0, has_side_effects=True, vmem_limit_bytes=40 * 1024 * 1024
+            collective_id=0, has_side_effects=True, vmem_limit_bytes=52 * 1024 * 1024
         ),
     )(u)
     return result[None, None]

time: 31.2 us -> 27.9 us (0.89)
  Pallas kernels: 28.9 us -> 26.8 us
  local copies, waits for them, and re-layouts: 2.2 us -> 0.97 us
    pallas_call x1, Pallas kernels: 28.9 us -> 26.8 us  [on_device(): pl.pallas_call(functools.partial(kernel, tm, windows), out_shape=jax.Shap...]
    unnamed x3 -> x1, local copies, waits for them, and re-layouts: 2.2 us -> 0.97 us
where the time goes in v3:
time: 27.9 us; the launch traced here: 27.7 us
  Pallas kernels  26.8 us (96%)
  local copies, waits for them, and re-layouts  0.97 us (3%)
    pallas_call x1, Pallas kernels, on_device(): pl.pallas_call(functools.partial(kernel, tm, windows), out_shape=jax.Shap...  26.8 us
    unnamed x1, local copies, waits for them, and re-layouts  0.97 us

profile of v3, /device:TPU:25, one launch (start us, length us, event | category | flops | bytes accessed | tf_op | source)
XLA Modules:
  0.0 27.7 jit_solution(14211350581056794773)
XLA Ops:
  0.0 26.8 %shard_map.17 = f32[2,2,256,256]{3,2,1,0:T(8,128)S(1)} custom-call(f32[2,2,256,256]{3,2,1,0:T(8,128)} %bitcast.3), custom_call_target="tpu_custom_call" | custom-call | tf_op jit(solution)/shard_map/pallas_call | solution.py:391
  26.8 1.0 %copy.3 = f32[1,1,2,2,256,256]{5,4,3,2,1,0:T(8,128)} copy(f32[1,1,2,2,256,256]{5,4,3,2,1,0:T(8,128)S(1)} %bitcast.2) | data formatting | bytes 2097152

commit v4 on v3

--- a/solution.py
+++ b/solution.py
@@ -103,6 +103,7 @@
     greet(mate)
     for o in range(1, nx):
         greet({"tm": ((x + o) % nx) * 2 + c})
+        greet({"tm": ((x + o) % nx) * 2 + (1 - c)})
 
     @pl.when(z > 0)
     def _():
@@ -119,11 +120,11 @@
     inner = (z > 0) & (z < last)
     @pl.when(inner)
     def _():
-        pl.semaphore_wait(barrier, nx + 2)
+        pl.semaphore_wait(barrier, 2 * nx + 1)
 
     @pl.when(jnp.logical_not(inner))
     def _():
-        pl.semaphore_wait(barrier, nx + 1)
+        pl.semaphore_wait(barrier, 2 * nx)
 
     def copy(src, dst, send, recv, to):
         return pltpu.make_async_remote_copy(
@@ -239,6 +240,10 @@
     def g_copy(j, core, k):
         ref = carry.at[:, piece(j * 2 + core, k), :]
         return copy(ref, ref, g_send.at[j, k], g_recv.at[j, k], mate)
+
+    def both_copy(to, k):
+        ref = carry.at[:, piece(d, k), :]
+        return copy(ref, ref, g_send.at[to, k], g_recv.at[x, k], {"tm": to * 2 + (1 - c)})
 
     def finish():
         before = pair(carry)
@@ -343,6 +348,8 @@
             z_copy(k, z).wait_recv()
             for j in others:
                 e_copy(x, j, k).start()
+                if k == chunks - 1:
+                    both_copy(j, k).start()
             g_copy(x, c, k).start()
 
             @pl.when(z < last)
@@ -353,7 +360,8 @@
         for k in range(chunks):
             for j in others:
                 e_copy(j, x, k).wait_recv()
-                g_copy(j, c, k).start()
+                if k < chunks - 1:
+                    g_copy(j, c, k).start()
 
         @pl.when(z == 1)
         def _():
@@ -367,7 +375,7 @@
         for k in range(chunks):
             for j in others:
                 e_copy(x, j, k).wait_send()
-                g_copy(j, c, k).wait_send()
+                (g_copy(j, c, k) if k < chunks - 1 else both_copy(j, k)).wait_send()
             g_copy(x, c, k).wait_send()
 
         @pl.when(z < last)

time: 27.9 us -> 27.5 us (0.986)
  Pallas kernels: 26.8 us -> 26.3 us
    pallas_call x1, Pallas kernels: 26.8 us -> 26.3 us  [on_device(): pl.pallas_call(functools.partial(kernel, tm, windows), out_shape=jax.Shap...]
where the time goes in v4:
time: 27.5 us; the launch traced here: 27.3 us
  Pallas kernels  26.3 us (96%)
  local copies, waits for them, and re-layouts  0.97 us (4%)
    pallas_call x1, Pallas kernels, on_device(): pl.pallas_call(functools.partial(kernel, tm, windows), out_shape=jax.Shap...  26.3 us
    unnamed x1, local copies, waits for them, and re-layouts  0.97 us

profile of v4, /device:TPU:25, one launch (start us, length us, event | category | flops | bytes accessed | tf_op | source)
XLA Modules:
  0.0 27.3 jit_solution(145846854380215244)
XLA Ops:
  0.0 26.3 %shard_map.17 = f32[2,2,256,256]{3,2,1,0:T(8,128)S(1)} custom-call(f32[2,2,256,256]{3,2,1,0:T(8,128)} %bitcast.3), custom_call_target="tpu_custom_call" | custom-call | tf_op jit(solution)/shard_map/pallas_call | solution.py:399
  26.4 1.0 %copy.3 = f32[1,1,2,2,256,256]{5,4,3,2,1,0:T(8,128)} copy(f32[1,1,2,2,256,256]{5,4,3,2,1,0:T(8,128)S(1)} %bitcast.2) | data formatting | bytes 2097152
